TPU v7x, 128 devices: a whole 4x4x4 slice. The times are simulated.
128 devices in a mesh: section: 4 (over x_lo, core), ctx: 8 (over x_hi, z), tp: 4 (over y).
Axes of the slice: x: 4 (x_hi: 2, x_lo: 2; x = x_hi * 2 + x_lo), y: 4, z: 4, core: 2. Of those that a mesh axis runs over, the one named last changes fastest.
Arguments:
- stretch_order: int32 [8, 2], replicated, may hold values from 0 to 15, as said below
- queries: bfloat16 [4, 4096, 2048], P('section', 'ctx', 'tp'), may hold values from -60 to 60
- key_rows: bfloat16 [4, 4096, 512], P('section', 'ctx', 'tp'), may hold values from -7 to 7
- value_rows: bfloat16 [4, 4096, 512], P('section', 'ctx', 'tp'), may hold values from -5 to 5
- out_grad: bfloat16 [4, 4096, 4096], P('section', ('ctx', 'tp')), may hold values from -6 to 6
- query_weight: bfloat16 [4, 4096, 2048], P('section', None, 'tp'), may hold values from -0.09375 to 0.09375
- key_weight: bfloat16 [4, 4096, 512], P('section', None, 'tp'), may hold values from -0.09375 to 0.09375
- value_weight: bfloat16 [4, 4096, 512], P('section', None, 'tp'), may hold values from -0.09375 to 0.09375
- output_weight: bfloat16 [4, 2048, 4096], P('section', 'tp'), may hold values from -0.125 to 0.125
Outputs:
- sent_grad: bfloat16 [4, 4096, 4096], P('section', ('ctx', 'tp'))
- key_grad: bfloat16 [4, 4096, 512], P('section', 'ctx', 'tp')
- value_grad: bfloat16 [4, 4096, 512], P('section', 'ctx', 'tp')
Inputs may be any that keep to these rules, and one draw needn't show every extreme that they name: `stretch_order`: row c lists the ids of the two blocks of 256 consecutive positions stored, in that order, at ctx index c; the two ids of a row sum to 15 and every id occurs once.
All inputs are finite; a program needn't handle non-finite values.
Results may differ from a plain program's by a relative error of at most 0.015.
Values may be sent and summed in bfloat16 or wider, within the bound.
No kernel may reach another device: no remote copies, remote signals or barrier semaphores. Data moves between devices by JAX's collectives and lax.ppermute only.
A program may use at most 128 MiB of HBM per device.

v0:
```python
import jax
import jax.numpy as jnp
from jax import lax
from jax.sharding import PartitionSpec as P

HD = 128
HQ = 16
KV = 4
NEG_LARGE = -1e30


def shifted(block, axis, distance):
    devices = range(lax.axis_size(axis))
    route = [((i - distance) % len(devices), i) for i in devices]
    return lax.ppermute(block, axis, route)


def contract_last(lhs, rhs):
    return lax.dot_general(lhs, rhs, (((1,), (1,)), ((), ())), preferred_element_type=jnp.float32)


def key_positions(flat_order, offset, row_count, block_len):
    row_ids = offset + jnp.arange(row_count, dtype=jnp.int32)
    owner = row_ids // block_len
    table = jnp.arange(flat_order.shape[0], dtype=jnp.int32)
    picked = jnp.sum(jnp.where(owner[:, None] == table[None, :], flat_order[None, :], 0), axis=1)
    return picked * block_len + row_ids % block_len


def block_scores(query_blk, grad_blk, key_blk, value_blk, score_scale):
    scores = (
        jnp.einsum("qghe,kge->ghqk", query_blk, key_blk, preferred_element_type=jnp.float32)
        * score_scale
    )
    grad_probs = jnp.einsum(
        "qghe,kge->ghqk", grad_blk, value_blk, preferred_element_type=jnp.float32
    )
    return (scores, grad_probs)


def stats_update(running, query_blk, grad_blk, query_pos, key_blk, value_blk, key_pos, score_scale):
    run_max, run_sum, run_dot = running
    scores, grad_probs = block_scores(query_blk, grad_blk, key_blk, value_blk, score_scale)
    visible = key_pos[None, :] <= query_pos[:, None]
    masked = jnp.where(visible, scores, NEG_LARGE)
    new_max = jnp.maximum(run_max, jnp.max(masked, axis=-1))
    weights = jnp.where(visible, jnp.exp(masked - new_max[..., None]), 0.0)
    factor = jnp.exp(run_max - new_max)
    new_sum = run_sum * factor + jnp.sum(weights, axis=-1)
    new_dot = run_dot * factor + jnp.sum(weights * grad_probs, axis=-1)
    return (new_max, new_sum, new_dot)


def block_grads(query_part, key_blk, value_blk, key_pos, score_scale):
    query_blk, grad_blk, query_pos, lse_blk, delta_blk = query_part
    scores, grad_probs = block_scores(query_blk, grad_blk, key_blk, value_blk, score_scale)
    visible = key_pos[None, :] <= query_pos[:, None]
    attn_probs = jnp.where(visible, jnp.exp(scores - lse_blk[..., None]), 0.0)
    dscore = attn_probs * (grad_probs - delta_blk[..., None])
    probs_low = attn_probs.astype(jnp.bfloat16)
    dscore_low = dscore.astype(jnp.bfloat16)
    results = []
    results.append(
        jnp.einsum("ghqk,kge->qghe", dscore_low, key_blk, preferred_element_type=jnp.float32)
        * score_scale
    )
    results.append(
        jnp.einsum("ghqk,qghe->kge", dscore_low, query_blk, preferred_element_type=jnp.float32)
        * score_scale
    )
    results.append(
        jnp.einsum("ghqk,qghe->kge", probs_low, grad_blk, preferred_element_type=jnp.float32)
    )
    return tuple(results)


def guarded(query_part, key_blk, value_blk, key_pos, score_scale, zero_like):

    def guarded_active(operands):
        return block_grads(query_part, operands[0], operands[1], operands[2], score_scale)

    def skipped(operands):
        return zero_like

    return lax.cond(
        jnp.min(key_pos) <= jnp.max(query_part[2]),
        guarded_active,
        skipped,
        (key_blk, value_blk, key_pos),
    )


def per_device(
    stretch_order,
    queries,
    key_rows,
    value_rows,
    out_grad,
    query_weight,
    key_weight,
    value_weight,
    output_weight,
):
    score_scale = HD ** (-0.5)
    group_len = HQ // KV
    query_mat = queries[0]
    key_mat = key_rows[0]
    value_mat = value_rows[0]
    tok_dev = query_mat.shape[0]
    block_len = tok_dev // 2
    kv_dev = key_mat.shape[1] // HD
    block_total = 2 * lax.axis_size("ctx")
    flat_order = stretch_order.reshape(-1)
    own_ids = lax.dynamic_slice_in_dim(flat_order, 2 * lax.axis_index("ctx"), 2, 0)
    out_weight = output_weight[0]
    attn_grad = contract_last(
        lax.all_gather(out_grad[0], "tp", axis=0, tiled=True), out_weight
    ).astype(jnp.bfloat16)
    query_four = query_mat.reshape(tok_dev, kv_dev, group_len, HD)
    grad_four = attn_grad.reshape(tok_dev, kv_dev, group_len, HD)
    local_pos = jnp.arange(block_len, dtype=jnp.int32)
    query_halves = []
    for half_idx in range(2):
        query_halves.append(
            (
                query_four[half_idx * block_len : (half_idx + 1) * block_len],
                grad_four[half_idx * block_len : (half_idx + 1) * block_len],
                own_ids[half_idx] * block_len + local_pos,
            )
        )

    def stats_add(running, key_blk, value_blk, key_pos):
        updated = []
        for half_idx in range(2):
            query_blk, grad_blk, query_pos = query_halves[half_idx]

            def stats_active(state):
                return stats_update(
                    state, query_blk, grad_blk, query_pos, key_blk, value_blk, key_pos, score_scale
                )

            def unchanged(state):
                return state

            updated.append(
                lax.cond(
                    jnp.min(key_pos) <= jnp.max(query_pos),
                    stats_active,
                    unchanged,
                    running[half_idx],
                )
            )
        return tuple(updated)

    stat_shape = (kv_dev, group_len, block_len)
    init_one = (
        jnp.full(stat_shape, NEG_LARGE, jnp.float32),
        jnp.zeros(stat_shape, jnp.float32),
        jnp.zeros(stat_shape, jnp.float32),
    )
    init_stats = (init_one, init_one)
    keys_all, values_all = (
        lax.all_gather(key_mat, "ctx", axis=0, tiled=True),
        lax.all_gather(value_mat, "ctx", axis=0, tiled=True),
    )
    keys_three = keys_all.reshape(-1, kv_dev, HD)
    values_three = values_all.reshape(-1, kv_dev, HD)
    seq_rows = keys_three.shape[0]

    def stats_step(block_idx, running):
        offset = block_idx * block_len
        key_blk = lax.dynamic_slice_in_dim(keys_three, offset, block_len, 0)
        value_blk = lax.dynamic_slice_in_dim(values_three, offset, block_len, 0)
        return stats_add(
            running, key_blk, value_blk, key_positions(flat_order, offset, block_len, block_len)
        )

    running = lax.fori_loop(0, block_total, stats_step, init_stats)
    full_parts = []
    for half_idx in range(2):
        run_max, run_sum, run_dot = running[half_idx]
        lse_blk = run_max + jnp.log(run_sum)
        delta_blk = run_dot / run_sum
        full_parts.append(query_halves[half_idx] + (lse_blk, delta_blk))
    zero_query = jnp.zeros((block_len, kv_dev, group_len, HD), jnp.float32)
    zero_keys = jnp.zeros((block_len, kv_dev, HD), jnp.float32)

    def grad_step(block_idx, state):
        query_sums, key_sums, value_sums = state
        offset = block_idx * block_len
        key_blk = lax.dynamic_slice_in_dim(keys_three, offset, block_len, 0)
        value_blk = lax.dynamic_slice_in_dim(values_three, offset, block_len, 0)
        key_pos = key_positions(flat_order, offset, block_len, block_len)
        key_add = zero_keys
        value_add = zero_keys
        new_query = []
        for half_idx in range(2):
            part_query, part_key, part_value = guarded(
                full_parts[half_idx],
                key_blk,
                value_blk,
                key_pos,
                score_scale,
                (zero_query, zero_keys, zero_keys),
            )
            new_query.append(query_sums[half_idx] + part_query)
            key_add = key_add + part_key
            value_add = value_add + part_value
        key_sums = lax.dynamic_update_slice_in_dim(
            key_sums, lax.dynamic_slice_in_dim(key_sums, offset, block_len, 0) + key_add, offset, 0
        )
        value_sums = lax.dynamic_update_slice_in_dim(
            value_sums,
            lax.dynamic_slice_in_dim(value_sums, offset, block_len, 0) + value_add,
            offset,
            0,
        )
        return (tuple(new_query), key_sums, value_sums)

    zero_full = jnp.zeros((seq_rows, kv_dev, HD), jnp.float32)
    query_sums, key_sums, value_sums = lax.fori_loop(
        0, block_total, grad_step, ((zero_query, zero_query), zero_full, zero_full)
    )
    key_own, value_own = (
        lax.psum_scatter(
            key_sums.astype(jnp.bfloat16), "ctx", scatter_dimension=0, tiled=True
        ).astype(jnp.float32),
        lax.psum_scatter(
            value_sums.astype(jnp.bfloat16), "ctx", scatter_dimension=0, tiled=True
        ).astype(jnp.float32),
    )
    query_grad = (
        jnp.concatenate(query_sums, axis=0)
        .reshape(tok_dev, kv_dev * group_len * HD)
        .astype(jnp.bfloat16)
    )
    key_grad = key_own.reshape(tok_dev, kv_dev * HD).astype(jnp.bfloat16)
    value_grad = value_own.reshape(tok_dev, kv_dev * HD).astype(jnp.bfloat16)
    query_mixer = query_weight[0]
    key_mixer = key_weight[0]
    value_mixer = value_weight[0]
    summed = contract_last(query_grad, query_mixer)
    summed = summed + contract_last(key_grad, key_mixer)
    summed = summed + contract_last(value_grad, value_mixer)
    input_grad = lax.psum_scatter(
        summed.astype(jnp.bfloat16), "tp", scatter_dimension=0, tiled=True
    )
    sent_grad = shifted(input_grad, "section", -1)
    return (sent_grad[None], key_grad[None], value_grad[None])


def solution(mesh):
    placed = (
        P(),
        P("section", "ctx", "tp"),
        P("section", "ctx", "tp"),
        P("section", "ctx", "tp"),
        P("section", ("ctx", "tp"), None),
        P("section", None, "tp"),
        P("section", None, "tp"),
        P("section", None, "tp"),
        P("section", "tp", None),
    )
    return jax.shard_map(
        per_device,
        mesh=mesh,
        in_specs=placed,
        out_specs=(
            P("section", ("ctx", "tp"), None),
            P("section", "ctx", "tp"),
            P("section", "ctx", "tp"),
        ),
        check_vma=False,
    )
```

profile of v0, /device:TPU:1, one launch (start us, length us, event | category | flops | bytes accessed | tf_op | source)
XLA Modules:
  0.0 694.0 jit_solution(15591792125867270716)
XLA Ops:
  15.3 45.6 %all-gather.11.cloned.1.call-done = bf16[1,512,4096]{2,1,0:T(8,128)(2,1)} async-done(((bf16[1,128,4096]{2,1,0:T(8,128)(2,1)}), bf16[1,512,4096]{2,1,0:T(8,128)(2,1)}) %all-gather.11.cloned.1.call-update) | async-done | bytes 4194320 | tf_op jit(solution)/shard_map/all_gather | solution.py:117
  60.9 5.8 fusion.75
  67.2 41.5 %all-gather.7.cloned.1.call-done = bf16[1,4096,128]{2,1,0:T(8,128)(2,1)} async-done(((bf16[1,512,128]{2,1,0:T(8,128)(2,1)}), bf16[1,4096,128]{2,1,0:T(8,128)(2,1)}) %all-gather.7.cloned.1.call-update) | async-done | bytes 1048592 | tf_op jit(solution)/shard_map/all_gather | solution.py:163
  108.6 47.6 %all-gather.9.cloned.1.call-done = bf16[1,4096,128]{2,1,0:T(8,128)(2,1)} async-done(((bf16[1,512,128]{2,1,0:T(8,128)(2,1)}), bf16[1,4096,128]{2,1,0:T(8,128)(2,1)}) %all-gather.9.cloned.1.call-update) | async-done | bytes 1048592 | tf_op jit(solution)/shard_map/all_gather | solution.py:164
  156.3 86.4 %while.50 = (s32[]{:T(128)}, f32[1,4,256]{2,1,0:T(4,128)S(1)}, f32[1,4,256]{2,1,0:T(4,128)S(1)}, f32[1,4,256]{2,1,0:T(4,128)S(1)}, f32[1,4,256]{2,1,0:T(4,128)S(...) while((s32[]{:T(128)}, f32[1,4,256]{2,1,0:T(4,128)S(1)}, ...), condition=%wide.wide.region_15.16_spmd.clone, body=%wide.wide.region_2.15_spmd.clone.sunk | while | flops 273836032 | bytes 8552063 | solution.py:178
  245.4 1.5 broadcast_in_dim.157
  246.9 218.1 %while.51 = (s32[]{:T(128)}, f32[256,1,4,128]{3,0,2,1:T(8,128)}, f32[256,1,4,128]{3,0,2,1:T(8,128)}, f32[4096,1,128]{2,0,1:T(8,128)}, f32[4096,1,128]{2,0,1:T(8,...) while((s32[]{:T(128)}, f32[256,1,4,128]{3,0,2,1:T(8,128)}, ...), condition=%wide.wide.region_23.24_spmd.clone, body=%wide.wide.region_16.0_spmd.clone.sunk | while | flops 675893248 | bytes 18251352 | solution.py:221
  252.4 2.4 conditional.18
  254.9 3.7 conditional.19
  259.7 1.8 add_dynamic-update-slice_fusion.4
  267.1 2.4 conditional.18
  271.0 2.3 select_add_fusion.4
  273.3 1.8 add_dynamic-update-slice_fusion.4
  280.7 2.4 conditional.18
  284.5 2.3 select_add_fusion.4
  286.8 1.8 add_dynamic-update-slice_fusion.4
  294.2 2.4 conditional.18
  298.1 2.3 select_add_fusion.4
  300.4 1.8 add_dynamic-update-slice_fusion.4
  309.3 2.3 select_add_fusion.4
  311.6 1.8 add_dynamic-update-slice_fusion.4
  319.0 2.4 conditional.18
  321.4 3.7 conditional.19
  325.2 2.3 select_add_fusion.4
  327.5 1.8 add_dynamic-update-slice_fusion.4
  334.9 2.4 conditional.18
  338.7 2.3 select_add_fusion.4
  341.0 1.8 add_dynamic-update-slice_fusion.4
  348.4 2.4 conditional.18
  352.3 2.3 select_add_fusion.4
  354.6 1.8 add_dynamic-update-slice_fusion.4
  362.0 2.4 conditional.18
  365.8 2.3 select_add_fusion.4
  368.2 1.8 add_dynamic-update-slice_fusion.4
  375.6 2.4 conditional.18
  379.4 2.3 select_add_fusion.4
  381.7 1.8 add_dynamic-update-slice_fusion.4
  389.1 2.4 conditional.18
  392.9 2.3 select_add_fusion.4
  395.3 1.9 add_dynamic-update-slice_fusion.4
  402.7 2.4 conditional.18
  406.5 2.3 select_add_fusion.4
  408.8 1.8 add_dynamic-update-slice_fusion.4
  417.7 2.3 select_add_fusion.4
  420.0 1.9 add_dynamic-update-slice_fusion.4
  427.4 2.4 conditional.18
  429.9 3.7 conditional.19
  433.6 2.3 select_add_fusion.4
  436.0 1.8 add_dynamic-update-slice_fusion.4
  444.8 2.3 select_add_fusion.4
  447.2 1.9 add_dynamic-update-slice_fusion.4
  454.6 2.4 conditional.18
  457.0 3.7 conditional.19
  460.8 2.3 select_add_fusion.4
  463.1 1.8 add_dynamic-update-slice_fusion.4
  464.9 2.8 convert_element_type.100
  467.8 2.7 convert_element_type.102
  471.0 7.8 %fusion.70 = f32[512,4096]{1,0:T(8,128)} fusion(bf16[1,4096,512]{2,1,0:T(8,128)(2,1)} %param.26, bf16[256,512]{0,1:T(8,128)(2,1)S(1)} %bitcast.275, bf16[256,512]{0,1:T(8,128)(2,1)S(1)} %bitcast.274), kind=kOutput, calls=%fused_computation.125 | convolution fusion | flops 2148532224 | bytes 13107200 | tf_op jit(solution)/shard_map/dot_general | solution.py:19
  478.8 60.4 %reduce-scatter.4.cloned.1.call-done = bf16[512,1,128]{2,0,1:T(8,128)(2,1)} async-done(((bf16[4096,1,128]{2,0,1:T(8,128)(2,1)}), bf16[512,1,128]{2,0,1:T(8,128)(2,1)}) %reduce-scatter.4.cloned.1.call-update) | async-done | bytes 131088 | tf_op jit(solution)/shard_map/reduce_scatter | solution.py:225
  539.2 5.4 fusion.81
  544.6 70.2 %reduce-scatter.6.cloned.1.call-done = bf16[512,1,128]{2,0,1:T(8,128)(2,1)} async-done(((bf16[4096,1,128]{2,0,1:T(8,128)(2,1)}), bf16[512,1,128]{2,0,1:T(8,128)(2,1)}) %reduce-scatter.6.cloned.1.call-update) | async-done | bytes 131088 | tf_op jit(solution)/shard_map/reduce_scatter | solution.py:228
  614.8 9.0 %add_convert_fusion = bf16[512,4096]{1,0:T(8,128)(2,1)} fusion(f32[512,4096]{1,0:T(8,128)} %fusion.70, f32[512,4096]{1,0:T(8,128)} %fusion.81, bf16[1,4096,128]{2,1,0:T(8,128)(2,1)S(1)} %copy-done.3, bf16[512,1,128]{2,0,1:T(8,128)(2,1)} %reduce-scatter.6.cloned.1.call-done), kind=kOutput, calls=%fused_computation.124 | convolution fusion | flops 543162368 | bytes 22151168 | tf_op jit(solution)/shard_map/dot_general | solution.py:19
  623.8 47.8 %reduce-scatter.8.cloned.1.call-done = bf16[128,4096]{1,0:T(8,128)(2,1)} async-done(((bf16[512,4096]{1,0:T(8,128)(2,1)}), bf16[128,4096]{1,0:T(8,128)(2,1)}) %reduce-scatter.8.cloned.1.call-update) | async-done | bytes 1048592 | tf_op jit(solution)/shard_map/reduce_scatter | solution.py:245
  672.4 13.8 %collective-permute-done = bf16[128,4096]{1,0:T(8,128)(2,1)S(1)} collective-permute-done((bf16[128,4096]{1,0:T(8,128)(2,1)}, bf16[128,4096]{1,0:T(8,128)(2,1)S(1)}, u32[]{:S(2)}, u32[]{:S(2)}) %collective-permute-start) | collective-permute-done | bytes 1048608 | tf_op jit(solution)/shard_map/ppermute | solution.py:15
  (608 shorter events, 203.8 us)
Async XLA Ops:
  7.2 532.0 %copy-start = (bf16[1,4096,128]{2,1,0:T(8,128)(2,1)S(1)}, bf16[1,4096,128]{2,1,0:T(8,128)(2,1)}, u32[]{:S(2)}) copy-start(bf16[1,4096,128]{2,1,0:T(8,128)(2,1)} %param.27) | copy-start | bytes 3145732
  7.2 53.8 %all-gather.11.cloned.1.call-start = ((), (), s32[]{:S(2)}) async-start(), calls=%async_computation.8 | async-start | bytes 5242880 | tf_op jit(solution)/shard_map/all_gather | solution.py:117
  7.9 100.7 %all-gather.7.cloned.1.call-start = ((), (), s32[]{:S(2)}) async-start(), calls=%async_computation.6 | async-start | bytes 1179648 | tf_op jit(solution)/shard_map/all_gather | solution.py:163
  8.7 147.6 %all-gather.9.cloned.1.call-start = ((), (), s32[]{:S(2)}) async-start(), calls=%async_computation.7 | async-start | bytes 1179648 | tf_op jit(solution)/shard_map/all_gather | solution.py:164
  9.4 529.8 %reduce-scatter.4.cloned.1.call-start = ((), (), s32[]{:S(2)}) async-start(), calls=%async_computation.3 | async-start | bytes 1179648 | tf_op jit(solution)/shard_map/reduce_scatter | solution.py:225
  10.2 56.6 %copy-start.4 = (s32[8,2]{1,0:T(8,128)}, s32[8,2]{1,0:T(8,128)S(1)}, u32[]{:S(2)}) copy-start(s32[8,2]{1,0:T(8,128)S(1)} %copy.48) | copy-start | bytes 196
  464.9 5.8 copy-start.2
  464.9 5.9 copy-start.1
  467.7 147.1 %reduce-scatter.6.cloned.1.call-start = ((), (), s32[]{:S(2)}) async-start(), calls=%async_computation.4 | async-start | bytes 1179648 | tf_op jit(solution)/shard_map/reduce_scatter | solution.py:228
  470.5 201.2 %reduce-scatter.8.cloned.1.call-start = ((), (), s32[]{:S(2)}) async-start(), calls=%async_computation.5 | async-start | bytes 5242880 | tf_op jit(solution)/shard_map/reduce_scatter | solution.py:245
  478.8 136.0 %copy-start.3 = (bf16[1,4096,128]{2,1,0:T(8,128)(2,1)S(1)}, bf16[1,4096,128]{2,1,0:T(8,128)(2,1)}, u32[]{:S(2)}) copy-start(bf16[1,4096,128]{2,1,0:T(8,128)(2,1)} %param.28) | copy-start | bytes 3145732
  671.7 14.5 %collective-permute-start = (bf16[128,4096]{1,0:T(8,128)(2,1)}, bf16[128,4096]{1,0:T(8,128)(2,1)S(1)}, u32[]{:S(2)}, u32[]{:S(2)}) collective-permute-start(bf16[128,4096]{1,0:T(8,128)(2,1)} %reduce-scatter.8.cloned.1.call-done), channel_id=1, source_target_pairs={{32,0},{64,32},{96,64},{0,96},{33,1},{65,33},{97,65},{1,97},{34,2}... | collective-permute-start | bytes 3145736 | tf_op jit(solution)/shard_map/ppermute | solution.py:15
Sparse Core Ops, SparseCore 0:
  9.6 51.2 all-gather.10
  63.3 45.3 all-gather.6
  111.0 45.1 all-gather.8
  467.8 71.2 reduce-scatter.3
  543.2 71.5 reduce-scatter.5
  624.0 47.6 reduce-scatter.7
where the time goes:
time: 699 us; the launch traced here: 694 us
  waiting for transfers between devices  329 us (47%)
  other arithmetic  114 us (16%)
  loops' own time  84.3 us (12%)
  matrix products  83.8 us (12%)
  local copies, waits for them, and re-layouts  66.5 us (10%)
  between operations  15.5 us (2%)
    reduce_scatter x1, waiting for transfers between devices, per_device(): lax.psum_scatter(value_sums.astype(jnp.bfloat16), 'ctx', scatter_dimensio...  70.2 us
    reduce_scatter x1, waiting for transfers between devices, per_device(): lax.psum_scatter(key_sums.astype(jnp.bfloat16), 'ctx', scatter_dimension=...  60.4 us
    reduce_scatter x1, waiting for transfers between devices, per_device(): lax.psum_scatter(summed.astype(jnp.bfloat16), 'tp', scatter_dimension=0,...  47.8 us
    all_gather x1, waiting for transfers between devices, per_device(): lax.all_gather(value_mat, 'ctx', axis=0, tiled=True)  47.6 us
    all_gather x1, waiting for transfers between devices, per_device(): lax.all_gather(out_grad[0], 'tp', axis=0, tiled=True)  45.6 us
    all_gather x1, waiting for transfers between devices, per_device(): lax.all_gather(key_mat, 'ctx', axis=0, tiled=True)  41.5 us
    another operation x1, loops' own time, per_device(): running = lax.fori_loop(0, block_total, stats_step, init_stats)  41.3 us
    another operation x1, loops' own time, per_device(): lax.fori_loop(0, block_total, grad_step, ((zero_query, zero_query), zero_...  40.8 us
  transfers between devices with their start and end apart: 7, of which 7 were waited for; matrix products, arithmetic and copies ran while one was open for 4% of the time, Pallas kernels for 0%

commit v1 on v0

--- a/solution.py
+++ b/solution.py
@@ -161,7 +161,9 @@
     init_stats = (init_one, init_one)
     keys_all, values_all = (
         lax.all_gather(key_mat, "ctx", axis=0, tiled=True),
-        lax.all_gather(value_mat, "ctx", axis=0, tiled=True),
+        jnp.concatenate(
+            lax.all_to_all(jnp.stack([value_mat] * lax.axis_size("ctx")), "ctx", 0, 0), axis=0
+        ),
     )
     keys_three = keys_all.reshape(-1, kv_dev, HD)
     values_three = values_all.reshape(-1, kv_dev, HD)

time: 699 us -> 657 us (0.940)
  waiting for transfers between devices: 329 us -> 273 us
  starting transfers between devices: 1.15 us -> 9.42 us
    all_gather x1 -> x0, waiting for transfers between devices: 47.6 us -> none  [per_device(): lax.all_gather(value_mat, 'ctx', axis=0, tiled=True)]
    all_to_all x0 -> x1, starting transfers between devices: none -> 8.31 us  [per_device(): lax.all_to_all(jnp.stack([value_mat] * lax.axis_size('ctx')), 'ctx', 0, 0)]
    all_gather x1, waiting for transfers between devices: 45.6 us -> 37.7 us  [per_device(): lax.all_gather(out_grad[0], 'tp', axis=0, tiled=True)]
  transfers between devices with their start and end apart: 7 -> 7, of which waited for: 7 -> 6; matrix products, arithmetic and copies ran while one was open for 4% -> 4% of each run, Pallas kernels for 0% -> 0%
where the time goes in v1:
time: 657 us; the launch traced here: 652 us
  waiting for transfers between devices  273 us (42%)
  other arithmetic  115 us (18%)
  loops' own time  88.9 us (14%)
  matrix products  83.6 us (13%)
  local copies, waits for them, and re-layouts  66.9 us (10%)
  between operations  15.2 us (2%)
  starting transfers between devices  9.42 us (1%)
    reduce_scatter x1, waiting for transfers between devices, per_device(): lax.psum_scatter(value_sums.astype(jnp.bfloat16), 'ctx', scatter_dimensio...  70.2 us
    reduce_scatter x1, waiting for transfers between devices, per_device(): lax.psum_scatter(key_sums.astype(jnp.bfloat16), 'ctx', scatter_dimension=...  60.7 us
    reduce_scatter x1, waiting for transfers between devices, per_device(): lax.psum_scatter(summed.astype(jnp.bfloat16), 'tp', scatter_dimension=0,...  47.8 us
    another operation x1, loops' own time, per_device(): running = lax.fori_loop(0, block_total, stats_step, init_stats)  43.6 us
    another operation x1, loops' own time, per_device(): lax.fori_loop(0, block_total, grad_step, ((zero_query, zero_query), zero_...  43.1 us
    all_gather x1, waiting for transfers between devices, per_device(): lax.all_gather(key_mat, 'ctx', axis=0, tiled=True)  41.4 us
    all_gather x1, waiting for transfers between devices, per_device(): lax.all_gather(out_grad[0], 'tp', axis=0, tiled=True)  37.7 us
    add x16, other arithmetic, grad_step(): new_query.append(query_sums[half_idx] + part_query)  35.9 us
  transfers between devices with their start and end apart: 7, of which 6 were waited for; matrix products, arithmetic and copies ran while one was open for 4% of the time, Pallas kernels for 0%

profile of v1, /device:TPU:1, one launch (start us, length us, event | category | flops | bytes accessed | tf_op | source)
XLA Modules:
  0.0 651.7 jit_solution(1541437944068220375)
XLA Ops:
  8.7 2.0 stack.3
  10.7 8.3 %all-to-all-start = ((bf16[8,512,128]{2,1,0:T(8,128)(2,1)}), bf16[8,512,128]{2,1,0:T(8,128)(2,1)}, u32[]{:S(2)}, u32[]{:S(2)}) async-start(bf16[8,512,128]{2,1,0:T(8,128)(2,1)} %stack.3), calls=%async_computation | async-start | bytes 2097152 | tf_op jit(solution)/shard_map/all_to_all | solution.py:165
  23.3 37.7 %all-gather.7.cloned.1.call-done = bf16[1,512,4096]{2,1,0:T(8,128)(2,1)} async-done(((bf16[1,128,4096]{2,1,0:T(8,128)(2,1)}), bf16[1,512,4096]{2,1,0:T(8,128)(2,1)}) %all-gather.7.cloned.1.call-update) | async-done | bytes 4194320 | tf_op jit(solution)/shard_map/all_gather | solution.py:117
  61.0 5.8 fusion.75
  67.2 41.4 %all-gather.5.cloned.1.call-done = bf16[1,4096,128]{2,1,0:T(8,128)(2,1)} async-done(((bf16[1,512,128]{2,1,0:T(8,128)(2,1)}), bf16[1,4096,128]{2,1,0:T(8,128)(2,1)}) %all-gather.5.cloned.1.call-update) | async-done | bytes 1048592 | tf_op jit(solution)/shard_map/all_gather | solution.py:163
  108.7 88.7 %while.50 = (s32[]{:T(128)}, f32[1,4,256]{2,1,0:T(4,128)S(1)}, f32[1,4,256]{2,1,0:T(4,128)S(1)}, f32[1,4,256]{2,1,0:T(4,128)S(1)}, f32[1,4,256]{2,1,0:T(4,128)S(...) while((s32[]{:T(128)}, f32[1,4,256]{2,1,0:T(4,128)S(1)}, ...), condition=%wide.wide.region_15.16_spmd.clone, body=%wide.wide.region_2.15_spmd.clone.sunk | while | flops 273836032 | bytes 8552063 | solution.py:180
  201.6 221.0 %while.51 = (s32[]{:T(128)}, f32[256,1,4,128]{3,0,2,1:T(8,128)}, f32[256,1,4,128]{3,0,2,1:T(8,128)}, f32[4096,1,128]{2,0,1:T(8,128)}, f32[4096,1,128]{2,0,1:T(8,...) while((s32[]{:T(128)}, f32[256,1,4,128]{3,0,2,1:T(8,128)}, ...), condition=%wide.wide.region_23.24_spmd.clone, body=%wide.wide.region_16.0_spmd.clone.sunk | while | flops 675893248 | bytes 18251352 | solution.py:223
  207.3 2.4 conditional.18
  209.7 3.8 conditional.19
  214.6 1.8 add_dynamic-update-slice_fusion.4
  222.3 2.4 conditional.18
  226.0 2.3 select_add_fusion.4
  228.4 1.8 add_dynamic-update-slice_fusion.4
  236.0 2.4 conditional.18
  239.8 2.3 select_add_fusion.4
  242.1 1.8 add_dynamic-update-slice_fusion.4
  249.7 2.4 conditional.18
  253.5 2.3 select_add_fusion.4
  255.9 1.8 add_dynamic-update-slice_fusion.4
  264.9 2.3 select_add_fusion.4
  267.3 1.8 add_dynamic-update-slice_fusion.4
  274.9 2.4 conditional.18
  277.3 3.8 conditional.19
  281.1 2.3 select_add_fusion.4
  283.4 1.8 add_dynamic-update-slice_fusion.4
  291.0 2.4 conditional.18
  294.8 2.3 select_add_fusion.4
  297.1 1.8 add_dynamic-update-slice_fusion.4
  304.7 2.4 conditional.18
  308.5 2.3 select_add_fusion.4
  310.8 1.8 add_dynamic-update-slice_fusion.4
  318.4 2.4 conditional.18
  322.2 2.3 select_add_fusion.4
  324.6 1.8 add_dynamic-update-slice_fusion.4
  332.2 2.4 conditional.18
  336.0 2.3 select_add_fusion.4
  338.3 1.8 add_dynamic-update-slice_fusion.4
  345.9 2.4 conditional.18
  349.7 2.3 select_add_fusion.4
  352.0 1.8 add_dynamic-update-slice_fusion.4
  359.6 2.4 conditional.18
  363.4 2.3 select_add_fusion.4
  365.8 1.8 add_dynamic-update-slice_fusion.4
  374.8 2.3 select_add_fusion.4
  377.2 1.8 add_dynamic-update-slice_fusion.4
  384.8 2.4 conditional.18
  387.2 3.8 conditional.19
  390.9 2.3 select_add_fusion.4
  393.3 1.8 add_dynamic-update-slice_fusion.4
  402.3 2.3 select_add_fusion.4
  404.6 1.9 add_dynamic-update-slice_fusion.4
  412.3 2.4 conditional.18
  414.7 3.8 conditional.19
  418.5 2.3 select_add_fusion.4
  420.8 1.8 add_dynamic-update-slice_fusion.4
  422.6 2.8 convert_element_type.100
  425.4 2.7 convert_element_type.102
  428.6 7.8 %fusion.70 = f32[512,4096]{1,0:T(8,128)} fusion(bf16[1,4096,512]{2,1,0:T(8,128)(2,1)} %param.26, bf16[256,512]{0,1:T(8,128)(2,1)S(1)} %bitcast.276, bf16[256,512]{0,1:T(8,128)(2,1)S(1)} %bitcast.275), kind=kOutput, calls=%fused_computation.125 | convolution fusion | flops 2148532224 | bytes 13107200 | tf_op jit(solution)/shard_map/dot_general | solution.py:19
  436.5 60.7 %reduce-scatter.4.cloned.1.call-done = bf16[512,1,128]{2,0,1:T(8,128)(2,1)} async-done(((bf16[4096,1,128]{2,0,1:T(8,128)(2,1)}), bf16[512,1,128]{2,0,1:T(8,128)(2,1)}) %reduce-scatter.4.cloned.1.call-update) | async-done | bytes 131088 | tf_op jit(solution)/shard_map/reduce_scatter | solution.py:227
  497.2 5.4 fusion.81
  502.6 70.2 %reduce-scatter.6.cloned.1.call-done = bf16[512,1,128]{2,0,1:T(8,128)(2,1)} async-done(((bf16[4096,1,128]{2,0,1:T(8,128)(2,1)}), bf16[512,1,128]{2,0,1:T(8,128)(2,1)}) %reduce-scatter.6.cloned.1.call-update) | async-done | bytes 131088 | tf_op jit(solution)/shard_map/reduce_scatter | solution.py:230
  572.8 9.0 %add_convert_fusion = bf16[512,4096]{1,0:T(8,128)(2,1)} fusion(f32[512,4096]{1,0:T(8,128)} %fusion.70, f32[512,4096]{1,0:T(8,128)} %fusion.81, bf16[1,4096,128]{2,1,0:T(8,128)(2,1)S(1)} %copy-done.3, bf16[512,1,128]{2,0,1:T(8,128)(2,1)} %reduce-scatter.6.cloned.1.call-done), kind=kOutput, calls=%fused_computation.124 | convolution fusion | flops 543162368 | bytes 22151168 | tf_op jit(solution)/shard_map/dot_general | solution.py:19
  581.8 47.8 %reduce-scatter.8.cloned.1.call-done = bf16[128,4096]{1,0:T(8,128)(2,1)} async-done(((bf16[512,4096]{1,0:T(8,128)(2,1)}), bf16[128,4096]{1,0:T(8,128)(2,1)}) %reduce-scatter.8.cloned.1.call-update) | async-done | bytes 1048592 | tf_op jit(solution)/shard_map/reduce_scatter | solution.py:247
  630.4 13.8 %collective-permute-done = bf16[128,4096]{1,0:T(8,128)(2,1)S(1)} collective-permute-done((bf16[128,4096]{1,0:T(8,128)(2,1)}, bf16[128,4096]{1,0:T(8,128)(2,1)S(1)}, u32[]{:S(2)}, u32[]{:S(2)}) %collective-permute-start) | collective-permute-done | bytes 1048608 | tf_op jit(solution)/shard_map/ppermute | solution.py:15
  (612 shorter events, 203.7 us)
Async XLA Ops:
  7.2 490.0 %copy-start = (bf16[1,4096,128]{2,1,0:T(8,128)(2,1)S(1)}, bf16[1,4096,128]{2,1,0:T(8,128)(2,1)}, u32[]{:S(2)}) copy-start(bf16[1,4096,128]{2,1,0:T(8,128)(2,1)} %param.27) | copy-start | bytes 3145732
  7.2 11.9 %copy-start.6 = (s32[8,2]{0,1:T(2,128)S(1)}, s32[8,2]{0,1:T(2,128)}, u32[]{:S(2)}) copy-start(s32[8,2]{0,1:T(2,128)} %param.21) | copy-start | bytes 196
  7.2 14.7 %copy-start.4 = (bf16[1,512,512]{2,1,0:T(8,128)(2,1)S(1)}, bf16[1,512,512]{2,1,0:T(8,128)(2,1)}, u32[]{:S(2)}) copy-start(bf16[1,512,512]{2,1,0:T(8,128)(2,1)} %param.22) | copy-start | bytes 1572868
  7.2 53.8 %all-gather.7.cloned.1.call-start = ((), (), s32[]{:S(2)}) async-start(), calls=%async_computation.8 | async-start | bytes 5242880 | tf_op jit(solution)/shard_map/all_gather | solution.py:117
  7.9 100.7 %all-gather.5.cloned.1.call-start = ((), (), s32[]{:S(2)}) async-start(), calls=%async_computation.7 | async-start | bytes 1179648 | tf_op jit(solution)/shard_map/all_gather | solution.py:163
  10.7 56.5 %all-to-all-start = ((bf16[8,512,128]{2,1,0:T(8,128)(2,1)}), bf16[8,512,128]{2,1,0:T(8,128)(2,1)}, u32[]{:S(2)}, u32[]{:S(2)}) async-start(bf16[8,512,128]{2,1,0:T(8,128)(2,1)} %stack.3), calls=%async_computation | async-start | bytes 2097152 | tf_op jit(solution)/shard_map/all_to_all | solution.py:165
  19.0 478.2 %reduce-scatter.4.cloned.1.call-start = ((), (), s32[]{:S(2)}) async-start(), calls=%async_computation.4 | async-start | bytes 1179648 | tf_op jit(solution)/shard_map/reduce_scatter | solution.py:227
  19.1 47.7 %copy-start.5 = (s32[8,2]{1,0:T(8,128)}, s32[8,2]{1,0:T(8,128)S(1)}, u32[]{:S(2)}) copy-start(s32[8,2]{1,0:T(8,128)S(1)} %copy.48) | copy-start | bytes 196
  422.6 5.7 copy-start.2
  422.6 5.9 copy-start.1
  425.4 147.4 %reduce-scatter.6.cloned.1.call-start = ((), (), s32[]{:S(2)}) async-start(), calls=%async_computation.5 | async-start | bytes 1179648 | tf_op jit(solution)/shard_map/reduce_scatter | solution.py:230
  428.1 201.6 %reduce-scatter.8.cloned.1.call-start = ((), (), s32[]{:S(2)}) async-start(), calls=%async_computation.6 | async-start | bytes 5242880 | tf_op jit(solution)/shard_map/reduce_scatter | solution.py:247
  436.5 136.3 %copy-start.3 = (bf16[1,4096,128]{2,1,0:T(8,128)(2,1)S(1)}, bf16[1,4096,128]{2,1,0:T(8,128)(2,1)}, u32[]{:S(2)}) copy-start(bf16[1,4096,128]{2,1,0:T(8,128)(2,1)} %param.28) | copy-start | bytes 3145732
  629.7 14.5 %collective-permute-start = (bf16[128,4096]{1,0:T(8,128)(2,1)}, bf16[128,4096]{1,0:T(8,128)(2,1)S(1)}, u32[]{:S(2)}, u32[]{:S(2)}) collective-permute-start(bf16[128,4096]{1,0:T(8,128)(2,1)} %reduce-scatter.8.cloned.1.call-done), channel_id=1, source_target_pairs={{32,0},{64,32},{96,64},{0,96},{33,1},{65,33},{97,65},{1,97},{34,2}... | collective-permute-start | bytes 3145736 | tf_op jit(solution)/shard_map/ppermute | solution.py:15
Sparse Core Ops, SparseCore 0:
  9.7 51.2 all-gather.6
  63.3 45.2 all-gather.4
  425.5 71.6 reduce-scatter.3
  501.2 71.5 reduce-scatter.5
  582.0 47.6 reduce-scatter.7
